TPU v7x, 256 devices: a whole 4x4x8 slice. The times are simulated.
256 devices in a mesh: ctx: 32 (over z, y_hi, core), head: 8 (over y_lo, x).
Axes of the slice: x: 4, y: 4 (y_hi: 2, y_lo: 2; y = y_hi * 2 + y_lo), z: 8, core: 2. Of those that a mesh axis runs over, the one named last changes fastest.
Arguments:
- query1: bfloat16 [16384, 6144], P('ctx', 'head'), may hold values from -6 to 6
- key1: bfloat16 [16384, 6144], P('ctx', 'head'), may hold values from -6 to 6
- value1: bfloat16 [16384, 6144], P('ctx', 'head'), may hold values from -50 to 50
- log_decay: float32 [16384, 64], P('ctx', 'head'), may hold values from -1 to 0
- out_weight: bfloat16 [6144, 3072], P('head'), may hold values from -0.078125 to 0.078125
- query2: bfloat16 [16384, 6144], P('ctx', 'head'), may hold values from -12 to 12
- key2: bfloat16 [16384, 6144], P('ctx', 'head'), may hold values from -6 to 6
- value2: bfloat16 [16384, 6144], P('ctx', 'head'), may hold values from -6 to 6
Outputs:
- linear_mixed: bfloat16 [16384, 3072], P(('ctx', 'head'))
- attended: bfloat16 [16384, 6144], P('ctx', 'head')
All inputs are finite; a program needn't handle non-finite values.
Results may differ from a plain program's by a relative error of at most 0.017.
Values may be sent and summed in bfloat16 or wider, within the bound.
A program may use at most 64 MiB of HBM per device.

v0:
```python
import math

import jax
import jax.numpy as jnp
from jax import lax
from jax.sharding import PartitionSpec as P

DH = 96
LBLOCK = 256


eps_norm = 1e-06


def passed_along(value, axis, steps):
    count = lax.axis_size(axis)
    initial, last = (max(0, -steps), min(count, count - steps))
    return lax.ppermute(value, axis, [(source, source + steps) for source in range(initial, last)])


def block_step(carry_state, pieces):
    query_part, key_part, value_part, decay_part = pieces
    block_len = decay_part.shape[0]
    running = jnp.cumsum(decay_part, axis=0)
    by_head = running.T
    gaps_log = by_head[:, :, None] - by_head[:, None, :]
    causal = jnp.arange(block_len)[:, None] >= jnp.arange(block_len)[None, :]
    weight = jnp.exp(jnp.where(causal[None], gaps_log, -jnp.inf))
    scores = jnp.einsum("ihd,jhd->hij", query_part, key_part, preferred_element_type=jnp.float32)
    mixing = (scores * weight).astype(jnp.bfloat16)
    inside = jnp.einsum("hij,jhd->ihd", mixing, value_part, preferred_element_type=jnp.float32)
    outside = jnp.einsum(
        "ihd,hde->ihe",
        query_part.astype(jnp.float32) * jnp.exp(running)[:, :, None],
        carry_state,
        precision=lax.Precision.HIGHEST,
    )
    block_total = running[-1]
    update = jnp.einsum(
        "jhd,jhe->hde",
        key_part.astype(jnp.float32) * jnp.exp(block_total[None, :] - running)[:, :, None],
        value_part.astype(jnp.float32),
        precision=lax.Precision.HIGHEST,
    )
    new_state = jnp.exp(block_total)[:, None, None] * carry_state + update
    return (new_state, inside + outside)


def per_device(query1, key1, value1, log_decay, out_weight, query2, key2, value2):
    tok_rows = query1.shape[0]
    head_count = log_decay.shape[1]
    head_size = DH
    block_count = tok_rows // LBLOCK
    inputs = (
        query1.reshape(block_count, LBLOCK, head_count, head_size),
        key1.reshape(block_count, LBLOCK, head_count, head_size),
        value1.reshape(block_count, LBLOCK, head_count, head_size),
        log_decay.reshape(block_count, LBLOCK, head_count),
    )
    empty_state = jnp.zeros((head_count, head_size, head_size), jnp.float32)
    state_dev, outputs = lax.scan(block_step, empty_state, inputs)
    local_out = outputs.reshape(tok_rows, head_count, head_size)
    decay_dev = jnp.cumsum(log_decay, axis=0)
    device_total = decay_dev[-1]
    position = lax.axis_index("ctx")
    totals = lax.all_gather(device_total[None, :], "ctx", axis=0, tiled=True)
    device_ids = jnp.arange(totals.shape[0], dtype=jnp.int32)[:, None]
    earlier_rows = device_ids < position
    running = jnp.cumsum(totals, axis=0)
    before_sum = jnp.sum(jnp.where(earlier_rows, totals, 0.0), axis=0)
    weights = jnp.exp(jnp.where(earlier_rows, before_sum[None, :] - running, -jnp.inf))
    incoming = empty_state + jnp.einsum(
        "nh,nhde->hde",
        weights,
        lax.all_gather(state_dev[None].astype(jnp.bfloat16), "ctx", axis=0, tiled=True).astype(
            jnp.float32
        ),
        precision=lax.Precision.HIGHEST,
    )
    correction = jnp.einsum(
        "ihd,hde->ihe",
        query1.reshape(tok_rows, head_count, head_size).astype(jnp.float32)
        * jnp.exp(decay_dev)[:, :, None],
        incoming,
        precision=lax.Precision.HIGHEST,
    )
    combined = local_out + correction
    mean_square = jnp.mean(combined * combined, axis=-1, keepdims=True)
    normed = (
        (combined / jnp.sqrt(mean_square + eps_norm))
        .astype(jnp.bfloat16)
        .reshape(tok_rows, head_count * head_size)
    )
    linear_mixed = lax.psum_scatter(
        jnp.dot(normed, out_weight, preferred_element_type=jnp.float32).astype(jnp.bfloat16),
        "head",
        scatter_dimension=0,
        tiled=True,
    )
    stacked = jnp.stack((key2, value2))
    received = []
    moving = stacked
    for distance in range(3):
        moving = passed_along(moving, "ctx", 1)
        received.append(moving)
    window_keys = jnp.concatenate([received[2], received[1], received[0], stacked], axis=1)
    heads_soft = query2.shape[1] // head_size
    query_rows = min(512, tok_rows)
    key_span = 3 * tok_rows + query_rows
    score_scale = 1.0 / math.sqrt(DH)
    lowest_key = (3 - position) * tok_rows

    def attend_block(block_index):
        first_row = block_index * query_rows
        query_part = query2.reshape(query_rows, heads_soft, head_size)
        key_part = window_keys[0].reshape(key_span, heads_soft, head_size)
        value_part = window_keys[1].reshape(key_span, heads_soft, head_size)
        scores = (
            jnp.einsum("ihd,jhd->hij", query_part, key_part, preferred_element_type=jnp.float32)
            * score_scale
        )
        query_pos = first_row + jnp.arange(query_rows, dtype=jnp.int32)[:, None]
        key_pos = first_row + jnp.arange(key_span, dtype=jnp.int32)[None, :]
        allowed = (
            (key_pos > query_pos) & (key_pos <= 3 * tok_rows + query_pos) & (key_pos >= lowest_key)
        )
        scores = jnp.where(allowed[None], scores, -jnp.inf)
        row_peak = jnp.max(scores, axis=-1, keepdims=True)
        exponent = jnp.exp(scores - row_peak)
        probability = (exponent / jnp.sum(exponent, axis=-1, keepdims=True)).astype(jnp.bfloat16)
        result = jnp.einsum(
            "hij,jhd->ihd", probability, value_part, preferred_element_type=jnp.float32
        )
        return result.astype(jnp.bfloat16).reshape(query_rows, heads_soft * head_size)

    attended = lax.map(attend_block, jnp.arange(tok_rows // query_rows, dtype=jnp.int32))
    attended = attended.reshape(tok_rows, heads_soft * head_size)
    return (linear_mixed, attended)


def solution(mesh):
    in_specs = (
        P("ctx", "head"),
        P("ctx", "head"),
        P("ctx", "head"),
        P("ctx", "head"),
        P("head", None),
        P("ctx", "head"),
        P("ctx", "head"),
        P("ctx", "head"),
    )
    out_specs = (P(("ctx", "head"), None), P("ctx", "head"))
    return jax.shard_map(
        per_device, mesh=mesh, in_specs=in_specs, out_specs=out_specs, check_vma=False
    )
```

profile of v0, /device:TPU:1, one launch (start us, length us, event | category | flops | bytes accessed | tf_op | source)
XLA Modules:
  0.0 302.6 jit_solution(10613626920884037711)
XLA Ops:
  7.2 2.2 reshape.198
  10.2 2.2 reshape.199
  13.1 3.0 reshape.200
  17.8 51.9 %while.4 = (s32[]{:T(128)}, f32[8,96,96]{2,1,0:T(8,128)S(1)}, f32[2,256,8,96]{1,0,3,2:T(2,128)}, f32[2,256,8]{1,2,0:T(8,128)}, bf16[2,256,8,96]{1,3,2,0:T(8,128)...) while((s32[]{:T(128)}, f32[8,96,96]{2,1,0:T(8,128)S(1)}, ...), condition=%wide.region_3.4_spmd.clone, body=%wide.region_0.3_spmd.clone.sunk | while | flops 658018304 | bytes 9203808 | solution.py:61
  26.1 16.7 %dynamic_update_slice.9 = f32[2,256,8,96]{1,0,3,2:T(2,128)} dynamic-update-slice(f32[2,256,8,96]{1,0,3,2:T(2,128)} %get-tuple-element.191, f32[1,256,8,96]{1,0,3,2:T(1,128)S(1)} %copy.94, s32[]{:T(128)} %get-tuple-element.189, s32[]{:T(128)} %constant.60.clone.1..sunk, s32[]{:T(128)} %constant.60.clone.1..sunk, s32[]{:T(128)} %constant.60.clone.1..sunk) | dynamic-update-slice | bytes 1572868 | tf_op jit(solution)/shard_map/while/body/jit(dynamic_update_index_in_dim)/dynamic_update_slice | solution.py:61
  52.0 16.7 %dynamic_update_slice.9 = f32[2,256,8,96]{1,0,3,2:T(2,128)} dynamic-update-slice(f32[2,256,8,96]{1,0,3,2:T(2,128)} %get-tuple-element.191, f32[1,256,8,96]{1,0,3,2:T(1,128)S(1)} %copy.94, s32[]{:T(128)} %get-tuple-element.189, s32[]{:T(128)} %constant.60.clone.1..sunk, s32[]{:T(128)} %constant.60.clone.1..sunk, s32[]{:T(128)} %constant.60.clone.1..sunk) | dynamic-update-slice | bytes 1572868 | tf_op jit(solution)/shard_map/while/body/jit(dynamic_update_index_in_dim)/dynamic_update_slice | solution.py:61
  70.5 2.7 pad_maximum_fusion
  73.2 6.2 %collective-permute-start = (bf16[2,512,768]{2,1,0:T(8,128)(2,1)}, bf16[2,512,768]{2,1,0:T(8,128)(2,1)}, u32[]{:S(2)}, u32[]{:S(2)}) collective-permute-start(bf16[2,512,768]{2,1,0:T(8,128)(2,1)} %pad_maximum_fusion), channel_id=1, source_target_pairs={{0,8},{8,16},{16,24},{24,32},{32,40},{40,48},{48,56},{56,64},{64,7... | collective-permute-start | bytes 4718600 | tf_op jit(solution)/shard_map/ppermute | solution.py:18
  79.7 2.2 reduce-window.16
  82.3 52.6 %all-gather.1 = f32[32,1,8]{2,1,0:T(1,128)S(1)} all-gather(f32[1,1,8]{2,1,0:T(1,128)S(1)} %bitcast.146), channel_id=1, replica_groups=mesh['ctx'=32,'head'=8] {'ctx'}, dimensions={0}, use_global_device_ids=true | all-gather | bytes 1056 | tf_op jit(solution)/shard_map/all_gather | solution.py:66
  135.0 2.5 reshape.184
  137.8 2.1 collective-permute-start.1
  139.9 45.3 %all-gather.4.cloned.1.call-done = bf16[256,96,96]{2,1,0:T(8,128)(2,1)} async-done(((bf16[8,96,96]{2,1,0:T(8,128)(2,1)}), bf16[256,96,96]{2,1,0:T(8,128)(2,1)}) %all-gather.4.cloned.1.call-update) | async-done | bytes 4718608 | tf_op jit(solution)/shard_map/all_gather | solution.py:75
  185.1 4.5 %multiply_reduce_fusion = f32[8,96,96]{2,1,0:T(8,128)S(1)} fusion(bf16[8,32,96,96]{3,2,0,1:T(8,128)(2,1)} %bitcast.131, f32[8,32]{0,1:T(8,128)S(1)} %exponential_bitcast_fusion), kind=kLoop, calls=%fused_computation.53 | loop fusion | flops 7004160 | bytes 5014528 | tf_op jit(solution)/shard_map/nh,nhde->hde/dot_general | solution.py:72
  191.5 6.4 %convolution_convert_fusion = bf16[512,3072]{1,0:T(8,128)(2,1)} fusion(bf16[512,768]{0,1:T(8,128)(2,1)S(1)} %bitcast.143, bf16[768,3072]{1,0:T(8,128)(2,1)} %param.14), kind=kOutput, calls=%fused_computation.57 | convolution fusion | flops 2417491968 | bytes 8650752 | tf_op jit(solution)/shard_map/dot_general | solution.py:95
  200.0 2.3 copy.65
  204.3 42.8 %collective-permute-done.2 = bf16[2,512,768]{2,1,0:T(8,128)(2,1)S(1)} collective-permute-done((bf16[2,512,768]{2,1,0:T(8,128)(2,1)}, bf16[2,512,768]{2,1,0:T(8,128)(2,1)S(1)}, u32[]{:S(2)}, u32[]{:S(2)}) %collective-permute-start.2) | collective-permute-done | bytes 1572896 | tf_op jit(solution)/shard_map/ppermute | solution.py:18
  247.1 2.8 maximum_maximum_fusion
  249.9 2.1 fusion.66
  252.0 4.7 %copy.64 = bf16[1,2048,768]{1,2,0:T(8,128)(2,1)} copy(bf16[1,2048,768]{2,1,0:T(8,128)(2,1)} %get-tuple-element.128) | data formatting | bytes 6291456 | tf_op jit(solution)/shard_map/while/body/eval_jaxpr/slice | solution.py:116
  256.7 3.0 copy.63
  259.7 14.4 %fusion.67 = f32[8,512]{1,0:T(8,128)S(1)} fusion(pred[512,2048]{0,1:T(8,128)(4,1)} %fusion.46, bf16[2048,8,96]{0,2,1:T(8,128)(2,1)} %bitcast.132, bf16[512,8,96]{0,2,1:T(8,128)(2,1)} %bitcast.140), kind=kOutput, calls=%fused_computation.85 | convolution fusion | flops 1644169216 | bytes 4997120 | tf_op jit(solution)/shard_map/while/body/eval_jaxpr/sub | solution.py:129
  274.2 19.3 %fusion.54 = bf16[8,96,512]{2,1,0:T(8,128)(2,1)} fusion(bf16[2048,8,96]{0,2,1:T(8,128)(2,1)S(1)} %bitcast.134, f32[8,512]{1,0:T(8,128)S(1)} %fusion.67, pred[512,2048]{0,1:T(8,128)(4,1)} %fusion.46, bf16[2048,8,96]{0,2,1:T(8,128)(2,1)} %bitcast.133, bf16[512,8,96]{0,2,1:T(8,128)(2,1)} %bitcast.141), kind=kOutput, calls=%fused_computation.67 | convolution fusion | flops 3263567872 | bytes 8929280 | tf_op jit(solution)/shard_map/while/body/eval_jaxpr/hij,jhd->ihd/dot_general | solution.py:131
  293.5 2.3 copy.67
  (72 shorter events, 29.2 us)
Async XLA Ops:
  7.2 178.0 %all-gather.4.cloned.1.call-start = ((), (), s32[]{:S(2)}) async-start(), calls=%async_computation.2 | async-start | bytes 6488064 | tf_op jit(solution)/shard_map/all_gather | solution.py:75
  19.3 0.6 copy-start.4
  45.2 0.6 copy-start.4
  69.7 9.7 %copy-start = (bf16[512,768]{1,0:T(8,128)(2,1)S(1)}, bf16[512,768]{1,0:T(8,128)(2,1)}, u32[]{:S(2)}) copy-start(bf16[512,768]{1,0:T(8,128)(2,1)} %param.10) | copy-start | bytes 2359300
  70.4 225.3 %reduce-scatter.2.cloned.1.call-start = ((), (), s32[]{:S(2)}) async-start(), calls=%async_computation.1 | async-start | bytes 3538944 | tf_op jit(solution)/shard_map/reduce_scatter | solution.py:94
  73.2 64.6 %collective-permute-start = (bf16[2,512,768]{2,1,0:T(8,128)(2,1)}, bf16[2,512,768]{2,1,0:T(8,128)(2,1)}, u32[]{:S(2)}, u32[]{:S(2)}) collective-permute-start(bf16[2,512,768]{2,1,0:T(8,128)(2,1)} %pad_maximum_fusion), channel_id=1, source_target_pairs={{0,8},{8,16},{16,24},{24,32},{32,40},{40,48},{48,56},{56,64},{64,7... | collective-permute-start | bytes 4718600 | tf_op jit(solution)/shard_map/ppermute | solution.py:18
  137.8 60.1 %collective-permute-start.1 = (bf16[2,512,768]{2,1,0:T(8,128)(2,1)}, bf16[2,512,768]{2,1,0:T(8,128)(2,1)}, u32[]{:S(2)}, u32[]{:S(2)}) collective-permute-start(bf16[2,512,768]{2,1,0:T(8,128)(2,1)} %collective-permute-done), channel_id=1, source_target_pairs={{0,8},{8,16},{16,24},{24,32},{32,40},{40,48},{48,56},{56,64},{64,7... | collective-permute-start | bytes 4718600 | tf_op jit(solution)/shard_map/ppermute | solution.py:18
  197.9 49.2 %copy-start.2 = (bf16[512,768]{1,0:T(8,128)(2,1)S(1)}, bf16[512,768]{1,0:T(8,128)(2,1)}, u32[]{:S(2)}) copy-start(bf16[512,768]{1,0:T(8,128)(2,1)} %param.17) | copy-start | bytes 2359300
  197.9 49.2 %copy-start.3 = (bf16[512,768]{1,0:T(8,128)(2,1)S(1)}, bf16[512,768]{1,0:T(8,128)(2,1)}, u32[]{:S(2)}) copy-start(bf16[512,768]{1,0:T(8,128)(2,1)} %param.16) | copy-start | bytes 2359300
  197.9 49.2 %collective-permute-start.2 = (bf16[2,512,768]{2,1,0:T(8,128)(2,1)}, bf16[2,512,768]{2,1,0:T(8,128)(2,1)S(1)}, u32[]{:S(2)}, u32[]{:S(2)}) collective-permute-start(bf16[2,512,768]{2,1,0:T(8,128)(2,1)} %collective-permute-done.1), channel_id=1, source_target_pairs={{0,8},{8,16},{16,24},{24,32},{32,40},{40,48},{48,56},{56,64},{64,7... | collective-permute-start | bytes 4718600 | tf_op jit(solution)/shard_map/ppermute | solution.py:18
  259.7 14.4 %copy-start.1 = (bf16[1,2048,768]{1,2,0:T(8,128)(2,1)S(1)}, bf16[1,2048,768]{1,2,0:T(8,128)(2,1)}, u32[]{:S(2)}) copy-start(bf16[1,2048,768]{1,2,0:T(8,128)(2,1)} %copy.63) | copy-start | bytes 9437188
Sparse Core Ops, SparseCore 0:
  70.5 114.5 all-gather.3
  198.0 39.6 reduce-scatter.1
where the time goes:
time: 306 us; the launch traced here: 303 us
  waiting for transfers between devices  88.1 us (29%)
  local copies, waits for them, and re-layouts  66.2 us (22%)
  blocking collectives  52.6 us (17%)
  matrix products  49.9 us (16%)
  other arithmetic  21 us (7%)
  between operations  14.2 us (5%)
  starting transfers between devices  10.4 us (3%)
    all_gather x1, blocking collectives, per_device(): totals = lax.all_gather(device_total[None, :], 'ctx', axis=0, tiled=True)  52.6 us
    all_gather x1, waiting for transfers between devices, per_device(): lax.all_gather(state_dev[None].astype(jnp.bfloat16), 'ctx', axis=0, tiled...  45.3 us
    ppermute x3, waiting for transfers between devices, passed_along(): lax.ppermute(value, axis, [(source, source + steps) for source in range(i...  42.9 us
    dynamic_update_slice x4, local copies, waits for them, and re-layouts, per_device(): state_dev, outputs = lax.scan(block_step, empty_state, inputs)  35 us
    dot_general x1, matrix products, attend_block(): jnp.einsum('hij,jhd->ihd', probability, value_part, preferred_element_typ...  19.3 us
    sub x1, matrix products, attend_block(): exponent = jnp.exp(scores - row_peak)  14.4 us
    ppermute x3, starting transfers between devices, passed_along(): lax.ppermute(value, axis, [(source, source + steps) for source in range(i...  10.3 us
    unnamed x14, local copies, waits for them, and re-layouts  7.93 us
  transfers between devices with their start and end apart: 5, of which 2 were waited for; matrix products, arithmetic and copies ran while one was open for 24% of the time, Pallas kernels for 0%

commit v1 on v0

v1 whole, which is shorter than its diff:
```python
import math

import jax
import jax.numpy as jnp
from jax import lax
from jax.experimental import pallas as pl
from jax.experimental.pallas import tpu as pltpu
from jax.sharding import PartitionSpec as P

DH = 96
ROWS = 512
COLS = 768
NH = 8
GW = 384
PROJ = 3072
HALF = PROJ // 2
WIN = 256
SPAN = 1792
NEG = -1e30
EPS = 1e-6
MESH = pl.DeviceIdType.MESH
F32 = jnp.float32
BF16 = jnp.bfloat16
HBM = pltpu.MemorySpace.HBM

HALO_FIRST = [(1, 0, 0)]
HALO_AFTER_A = [(0, 0, 0)]
HALO_AFTER_B = [(1, 1, 0)]
HALO_AFTER_C = [(0, 1, 0), (1, 0, 1), (0, 0, 1), (0, 1, 1), (1, 1, 1)]


def dot(a, b, ca, cb):
    return lax.dot_general(a, b, (((ca,), (cb,)), ((), ())), preferred_element_type=F32)


def lanes(shape):
    return lax.broadcasted_iota(jnp.int32, shape, len(shape) - 1)


def rows_of(shape):
    return lax.broadcasted_iota(jnp.int32, shape, len(shape) - 2)


def head_window(h):
    start = GW * lax.div(h, 4) + 128 * lax.div(lax.rem(h, 4), 2)
    return pl.multiple_of(start, 128), DH * h - start


def head_mask(low):
    lane = lanes((1, WIN))
    return (lane >= low) & (lane < low + DH)


def same_head(tile):
    row = lax.div(rows_of((GW, 128)), DH)
    col = lax.div(lanes((GW, 128)) + 128 * tile, DH)
    return row == col


def kernel(
    q1h, k1h, v1h, dec, wh, q2h, k2h, v2h,
    lin_out, att_out,
    q1, k1, v1, q2, kk, vv, w,
    dpad, crow, ct, cexp, acc, fold, dtot,
    recv_a, dec_a, tot_b, dec_s, recv_b, dec_b, pacc, send_c, recv_c,
    normed, part, x1s, x1r, x2s, x2r, ys, yr,
    s_scr, p_scr,
    load_sem, halo_send, halo_recv, fwd_send, a_send, a_recv, b_send, b_recv, c_send, c_recv,
    x_send, x_recv, y_send, y_recv,
):
    t, hd = lax.axis_index("ctx"), lax.axis_index("head")
    z, j, core = lax.div(t, 4), lax.rem(t, 4), lax.rem(t, 2)
    yl, x = lax.div(hd, 4), lax.rem(hd, 4)
    sibling = t + 1 - 2 * core
    x_up, x_down = yl * 4 + lax.rem(x + 1, 4), yl * 4 + lax.rem(x + 3, 4)
    y_other = (1 - yl) * 4 + x

    related = [
        (lax.rem(t + 2, 32), hd),
        (lax.rem(t + 30, 32), hd),
        (sibling, hd),
        (lax.rem(t + 29 + 6 * core, 32), hd),
        (t, x_up),
        (t, x_down),
        (t, y_other),
    ]
    related += [(4 * z + lax.rem(j + d, 4), hd) for d in (1, 2, 3)]
    related += [(lax.rem(t + 4 * d, 32), hd) for d in range(1, 8)]
    barrier = pltpu.get_barrier_semaphore()
    for device in related:
        pl.semaphore_signal(barrier, inc=1, device_id=device, device_id_type=MESH)

    own = pl.ds(3 * ROWS, ROWS)
    loads = [
        pltpu.make_async_copy(src, dst, load_sem.at[i])
        for i, (src, dst) in enumerate(
            [(k1h, k1), (v1h, v1), (q1h, q1), (q2h, q2), (k2h, kk.at[own]), (v2h, vv.at[own]), (wh, w)]
        )
    ]
    for copy in loads:
        copy.start()
    pl.semaphore_wait(barrier, len(related))

    def half(g):
        return pl.ds(GW * g, GW)

    def halo(kind, kv, g):
        src, dst = ((k2h, kk), (v2h, vv))[kv]
        slot = 1 if kind == 0 else 2 - 2 * core
        target = lax.rem(t + 2, 32) if kind == 0 else lax.rem(t + 1 + 2 * core, 32)
        return pltpu.make_async_remote_copy(
            src_ref=src.at[:, half(g)],
            dst_ref=dst.at[pl.ds(slot * ROWS, ROWS), half(g)],
            send_sem=halo_send.at[kind, kv, g],
            recv_sem=halo_recv.at[slot, kv, g],
            device_id=(target, hd),
            device_id_type=MESH,
        )

    def arrived(slot, kv, g):
        dst = (kk, vv)[kv].at[pl.ds(slot * ROWS, ROWS), half(g)]
        return pltpu.make_async_remote_copy(
            src_ref=dst,
            dst_ref=dst,
            send_sem=halo_send.at[0, kv, g],
            recv_sem=halo_recv.at[slot, kv, g],
            device_id=(sibling, hd),
            device_id_type=MESH,
        )

    def forward(kv, g):
        buf = (kk, vv)[kv]
        slot = 2 * core
        return pltpu.make_async_remote_copy(
            src_ref=buf.at[pl.ds(ROWS, ROWS), half(g)],
            dst_ref=buf.at[pl.ds(slot * ROWS, ROWS), half(g)],
            send_sem=fwd_send.at[kv, g],
            recv_sem=halo_recv.at[slot, kv, g],
            device_id=(sibling, hd),
            device_id_type=MESH,
        )

    for item in HALO_FIRST:
        halo(*item).start()

    dpad[...] = jnp.zeros_like(dpad)
    dpad[:, :NH] = dec[...]
    lower = (rows_of((ROWS, ROWS)) >= lanes((ROWS, ROWS))).astype(F32)
    running = lax.dot_general(
        lower, dpad[...], (((1,), (0,)), ((), ())), precision=lax.Precision.HIGHEST, preferred_element_type=F32
    )
    ct[...] = jnp.transpose(running)[:NH, :]
    for h in range(NH):
        crow[h] = jnp.broadcast_to(running[:, h : h + 1], (ROWS, 128))
    for h in range(NH):
        dtot[h : h + 1, :] = crow[h, ROWS - 1 : ROWS, :]
    lane = lanes((ROWS, 128))
    for g in range(2):
        for tile, cut in enumerate((96, 64, 32)):
            h = 4 * g + tile
            at = pl.ds(GW * g + 128 * tile, 128)
            cexp[:, at] = jnp.where(lane < cut, crow[h], crow[h + 1])

    loads[0].wait()
    loads[1].wait()
    for g in range(2):
        c = cexp[:, half(g)]
        kw = (k1[:, half(g)].astype(F32) * jnp.exp(cexp[ROWS - 1 : ROWS, half(g)] - c)).astype(BF16)
        full = dot(kw, v1[:, half(g)], 0, 0)
        total = jnp.zeros((GW, 128), F32)
        for tile in range(3):
            total += jnp.where(same_head(tile), full[:, 128 * tile : 128 * tile + 128], 0.0)
        fold[pl.ds(GW * g, GW), :] = total.astype(BF16)

    def two_heads(index):
        return pl.ds(pl.multiple_of(192 * index, 16), 192)

    a_copies = []
    for d in (1, 2, 3):
        to = lax.rem(j + d, 4)
        for n, (src, dst) in enumerate([(fold.at[two_heads(to)], recv_a.at[d]), (dtot, dec_a.at[d])]):
            copy = pltpu.make_async_remote_copy(
                src_ref=src, dst_ref=dst, send_sem=a_send.at[d, n], recv_sem=a_recv.at[d, n],
                device_id=(4 * z + to, hd), device_id_type=MESH,
            )
            copy.start()
            a_copies.append(copy)
    recv_a[0] = fold[two_heads(j), :]
    dec_a[0] = dtot[...]
    for item in HALO_AFTER_A:
        halo(*item).start()

    acc[...] = jnp.zeros_like(acc)
    loads[2].wait()
    tri = rows_of((256, 256)) >= lanes((256, 256))

    def intra(h, _):
        start, low = head_window(h)
        window = pl.ds(start, WIN)
        mask = head_mask(low)
        keep = mask.astype(F32).astype(BF16)
        qw = q1[:, window] * keep
        kw = k1[:, window]
        vw = v1[:, window]
        s0 = dot(qw[:256], kw[:256], 1, 1)
        s1 = dot(qw[256:], kw, 1, 1)
        ci = crow[h]
        ci = jnp.concatenate([ci, ci], axis=1)
        cj = ct[pl.ds(h, 1), :]
        e0 = jnp.exp(jnp.where(tri, ci[:256] - cj[:, :256], NEG))
        e10 = jnp.exp(ci[256:] - cj[:, :256])
        e11 = jnp.exp(jnp.where(tri, ci[256:] - cj[:, 256:], NEG))
        m0 = (s0 * e0).astype(BF16)
        m1 = (s1 * jnp.concatenate([e10, e11], axis=1)).astype(BF16)
        acc[pl.ds(0, 256), window] = jnp.where(mask, dot(m0, vw[:256], 1, 0), acc[pl.ds(0, 256), window])
        acc[pl.ds(256, 256), window] = jnp.where(mask, dot(m1, vw, 1, 0), acc[pl.ds(256, 256), window])
        return 0

    lax.fori_loop(0, NH // 2, intra, 0)

    for copy in a_copies:
        copy.wait_recv()

    def member(i):
        return lax.rem(j + 4 - i, 4)

    def head_rows(hh):
        return slice(DH * hh, DH * hh + DH)

    for hh in range(2):
        total = jnp.zeros((DH, 128), F32)
        for i in range(4):
            decay = jnp.exp(dec_a[member(i), pl.ds(2 * j + hh, 1), :])
            total = decay * total + recv_a[member(i), head_rows(hh), :].astype(F32)
        tot_b[head_rows(hh), :] = total.astype(BF16)
    dec_s[...] = dec_a[0] + dec_a[1] + dec_a[2] + dec_a[3]
    b_copies = []
    for d in range(1, 8):
        pair = []
        for n, (src, dst) in enumerate([(tot_b, recv_b.at[d]), (dec_s, dec_b.at[d])]):
            pair.append(
                pltpu.make_async_remote_copy(
                    src_ref=src, dst_ref=dst, send_sem=b_send.at[d, n], recv_sem=b_recv.at[d, n],
                    device_id=(lax.rem(t + 4 * d, 32), hd), device_id_type=MESH,
                )
            )
        b_copies.append(pair)

        @pl.when(z + d < 8)
        def _(pair=pair):
            for copy in pair:
                copy.start()

    for item in HALO_AFTER_B:
        halo(*item).start()

    lax.fori_loop(NH // 2, NH, intra, 0)

    for d in range(1, 8):

        @pl.when(z >= d)
        def _(pair=b_copies[d - 1]):
            for copy in pair:
                copy.wait_recv()

    pacc[...] = jnp.zeros_like(pacc)
    for zz in range(7):

        @pl.when(zz < z)
        def _(zz=zz):
            slot = lax.rem(z + 8 - zz, 8)
            for hh in range(2):
                decay = jnp.exp(dec_b[slot, pl.ds(2 * j + hh, 1), :])
                pacc[head_rows(hh), :] = decay * pacc[head_rows(hh), :] + recv_b[slot, head_rows(hh), :].astype(F32)

    for hh in range(2):
        state = pacc[head_rows(hh), :]
        for i in range(4):
            send_c[i, head_rows(hh), :] = state.astype(BF16)
            decay = jnp.exp(dec_a[member(i), pl.ds(2 * j + hh, 1), :])
            state = decay * state + recv_a[member(i), head_rows(hh), :].astype(F32)
    c_copies = []
    for d in (1, 2, 3):
        to = lax.rem(j + d, 4)
        copy = pltpu.make_async_remote_copy(
            src_ref=send_c.at[to], dst_ref=recv_c.at[j], send_sem=c_send.at[d], recv_sem=c_recv.at[d],
            device_id=(4 * z + to, hd), device_id_type=MESH,
        )
        copy.start()
        c_copies.append(copy)
    recv_c[j] = send_c[j]
    for item in HALO_AFTER_C:
        halo(*item).start()
    loads[6].wait()
    for copy in c_copies:
        copy.wait_recv()

    for g in range(2):
        states = jnp.concatenate([recv_c[2 * g], recv_c[2 * g + 1]], axis=0).astype(F32)
        wide = jnp.concatenate([jnp.where(same_head(i), states, 0.0).astype(BF16) for i in range(3)], axis=1)
        ones = jnp.concatenate([same_head(i).astype(F32).astype(BF16) for i in range(3)], axis=1)
        both = dot(q1[:, half(g)], wide, 1, 0) * jnp.exp(cexp[:, half(g)]) + acc[:, half(g)]
        square = both * both
        high = square.astype(BF16)
        rest = (square - high.astype(F32)).astype(BF16)
        mean = (dot(high, ones, 1, 0) + dot(rest, ones, 1, 0)) * (1.0 / DH)
        normed[:, half(g)] = (both * lax.rsqrt(mean + EPS)).astype(BF16)

    left, right = pl.ds(0, HALF), pl.ds(HALF, HALF)

    def project(d, cols):
        xt = lax.rem(x + d, 4)
        a = jnp.concatenate(
            [
                normed[pl.ds(pl.multiple_of(64 * xt, 64), 64), :],
                normed[pl.ds(pl.multiple_of(256 + 64 * xt, 64), 64), :],
            ],
            axis=0,
        )
        return dot(a, w[:, cols], 1, 0)

    def x_copy(n, src, dst, to):
        return pltpu.make_async_remote_copy(
            src_ref=src, dst_ref=dst, send_sem=x_send.at[n], recv_sem=x_recv.at[n],
            device_id=(t, to), device_id_type=MESH,
        )

    x1 = [x_copy(0, x1s.at[0], x1r.at[0], x_up), x_copy(1, x1s.at[1], x1r.at[1], x_down)]
    x2a = [
        x_copy(2, x2s.at[0, :, right], x2r.at[0, :, right], x_up),
        x_copy(3, x2s.at[1, :, left], x2r.at[1, :, left], x_down),
    ]
    x2b = [
        x_copy(4, x2s.at[0, :, left], x2r.at[0, :, left], x_up),
        x_copy(5, x2s.at[1, :, right], x2r.at[1, :, right], x_down),
    ]
    step = 512

    def cols_at(i):
        return pl.ds(pl.multiple_of(step * i, step), step)

    for side in range(2):

        def opposite(i, _, side=side):
            x1s[side, :, cols_at(i)] = project(2, cols_at(i + 3 * side)).astype(BF16)
            return 0

        lax.fori_loop(0, 3, opposite, 0)
        x1[side].start()
    for side in range(2):

        def alone(i, _, side=side):
            cols = cols_at(i + 3 * (1 - side))
            x2s[side, :, cols] = project(1 + 2 * side, cols).astype(BF16)
            return 0

        lax.fori_loop(0, 3, alone, 0)
        x2a[side].start()
    for side in range(2):

        def kept(i, _, side=side):
            part[1 + side, :, cols_at(i)] = project(1 + 2 * side, cols_at(i + 3 * side))
            return 0

        lax.fori_loop(0, 3, kept, 0)

    def own_rows(i, _):
        value = project(0, cols_at(i))
        part[3 + lax.div(i, 3), :, cols_at(lax.rem(i, 3))] = value
        return 0

    lax.fori_loop(0, 6, own_rows, 0)

    def second_step():
        for side in range(2):
            x1[side].wait_recv()

            def add(i, _, side=side):
                total = part[1 + side, :, cols_at(i)] + x1r[side, :, cols_at(i)].astype(F32)
                x2s[side, :, cols_at(i + 3 * side)] = total.astype(BF16)
                return 0

            lax.fori_loop(0, 3, add, 0)
            x2b[side].start()

    y_copies = [
        pltpu.make_async_remote_copy(
            src_ref=ys.at[i], dst_ref=yr.at[i], send_sem=y_send.at[i], recv_sem=y_recv.at[i],
            device_id=(t, y_other), device_id_type=MESH,
        )
        for i in range(2)
    ]
    mine_rows = pl.ds(pl.multiple_of(64 * yl, 64), 64)
    their_rows = pl.ds(pl.multiple_of(64 * (1 - yl), 64), 64)

    def third_step():
        for i in range(2):
            if i == 0:
                x2b[0].wait_recv()
                x2a[1].wait_recv()
            else:
                x2a[0].wait_recv()
                x2b[1].wait_recv()

            def add(n, _, i=i):
                cols = cols_at(n + 3 * i)

                def total(rows):
                    return (
                        part[3 + i, rows, cols_at(n)]
                        + x2r[0, rows, cols].astype(F32)
                        + x2r[1, rows, cols].astype(F32)
                    )

                ys[i, :, cols_at(n)] = total(their_rows).astype(BF16)
                part[3 + i, mine_rows, cols_at(n)] = total(mine_rows)
                return 0

            lax.fori_loop(0, 3, add, 0)
            y_copies[i].start()

    def pass_on(g):
        for kv in range(2):
            arrived(1, kv, g).wait_recv()
            forward(kv, g).start()

    def need(g):
        for kv in range(2):
            for slot in (0, 2):
                arrived(slot, kv, g).wait_recv()

    scale = (1.0 / math.sqrt(DH)) * math.log2(math.e)
    upper = lanes((256, 256)) > rows_of((256, 256))

    def attend(h, _):
        start, low = head_window(h)
        window = pl.ds(start, WIN)
        mask = head_mask(low)
        keep = mask.astype(F32).astype(BF16)
        for i in range(2):
            keys = pl.ds(256 * i, SPAN)
            qw = q2[pl.ds(256 * i, 256), window] * keep
            s_scr[i] = dot(qw, kk[keys, window], 1, 1)
            tops = []
            for n in range(7):
                cols = pl.ds(256 * n, 256)
                if n == 0:
                    s_scr[i, :, cols] = jnp.where(upper, s_scr[i, :, cols], NEG)
                if n == 6:
                    s_scr[i, :, cols] = jnp.where(tri, s_scr[i, :, cols], NEG)
                block = s_scr[i, :, cols]
                top = jnp.maximum(block[:, :128], block[:, 128:])
                first = 3 - (i + n) // 2
                if first > 0:
                    top = jnp.minimum(top, jnp.where(t >= first, 1e38, -1e38))
                tops.append(top)
            while len(tops) > 1:
                tops = [jnp.maximum(*tops[n : n + 2]) if n + 1 < len(tops) else tops[n] for n in range(0, len(tops), 2)]
            peak = jnp.max(tops[0], axis=1, keepdims=True) * scale
            total = jnp.zeros((256, 128), F32)
            for n in range(7):
                cols = pl.ds(256 * n, 256)
                first = 3 - (i + n) // 2
                shift = peak + jnp.where(t >= first, 0.0, 1e30) if first > 0 else peak
                e = jnp.exp2(s_scr[i, :, cols] * scale - shift)
                total += e[:, :128] + e[:, 128:]
                p_scr[i, :, cols] = e.astype(BF16)
            out = dot(p_scr[i], vv[keys, window], 1, 0) * (1.0 / jnp.sum(total, axis=1, keepdims=True))
            rows = pl.ds(256 * i, 256)
            old = att_out[rows, window].astype(F32)
            att_out[rows, window] = jnp.where(mask, out, old).astype(BF16)
        return 0

    att_out[...] = jnp.zeros_like(att_out)
    for i in (3, 4, 5):
        loads[i].wait()
    pass_on(0)
    need(0)
    lax.fori_loop(0, 2, attend, 0)
    second_step()
    lax.fori_loop(2, 4, attend, 0)
    pass_on(1)
    need(1)
    lax.fori_loop(4, 6, attend, 0)
    third_step()
    lax.fori_loop(6, 8, attend, 0)

    for i in range(2):
        y_copies[i].wait_recv()
        for n in range(3):
            cols = pl.ds(step * n, step)
            total = part[3 + i, mine_rows, cols] + yr[i, :, cols].astype(F32)
            lin_out[:, pl.ds(HALF * i + step * n, step)] = total.astype(BF16)

    for item in HALO_FIRST + HALO_AFTER_A + HALO_AFTER_B + HALO_AFTER_C:
        halo(*item).wait_send()
    for g in range(2):
        for kv in range(2):
            forward(kv, g).wait_send()
    for copy in a_copies + c_copies + x1 + x2a + x2b + y_copies:
        copy.wait_send()
    for d in range(1, 8):

        @pl.when(z + d < 8)
        def _(pair=b_copies[d - 1]):
            for copy in pair:
                copy.wait_send()


def per_device(query1, key1, value1, log_decay, out_weight, query2, key2, value2):
    vm = pltpu.VMEM
    dma = pltpu.SemaphoreType.DMA
    hbm = pl.BlockSpec(memory_space=HBM)
    vmem = pl.BlockSpec(memory_space=vm)
    return pl.pallas_call(
        kernel,
        out_shape=(
            jax.ShapeDtypeStruct((64, PROJ), BF16),
            jax.ShapeDtypeStruct((ROWS, COLS), BF16),
        ),
        in_specs=[hbm, hbm, hbm, vmem, hbm, hbm, hbm, hbm],
        out_specs=(vmem, vmem),
        scratch_shapes=[
            vm((ROWS, COLS), BF16),
            vm((ROWS, COLS), BF16),
            vm((ROWS, COLS), BF16),
            vm((ROWS, COLS), BF16),
            vm((4 * ROWS, COLS), BF16),
            vm((4 * ROWS, COLS), BF16),
            vm((COLS, PROJ), BF16),
            vm((ROWS, 128), F32),
            vm((NH, ROWS, 128), F32),
            vm((NH, ROWS), F32),
            vm((ROWS, COLS), F32),
            vm((ROWS, COLS), F32),
            vm((COLS, 128), BF16),
            vm((NH, 128), F32),
            vm((4, 192, 128), BF16),
            vm((4, NH, 128), F32),
            vm((192, 128), BF16),
            vm((NH, 128), F32),
            vm((8, 192, 128), BF16),
            vm((8, NH, 128), F32),
            vm((192, 128), F32),
            vm((4, 192, 128), BF16),
            vm((4, 192, 128), BF16),
            vm((ROWS, COLS), BF16),
            vm((5, 128, HALF), F32),
            vm((2, 128, HALF), BF16),
            vm((2, 128, HALF), BF16),
            vm((2, 128, PROJ), BF16),
            vm((2, 128, PROJ), BF16),
            vm((2, 64, HALF), BF16),
            vm((2, 64, HALF), BF16),
            vm((2, 256, SPAN), F32),
            vm((2, 256, SPAN), BF16),
            dma((7,)),
            dma((2, 2, 2)),
            dma((3, 2, 2)),
            dma((2, 2)),
            dma((4, 2)),
            dma((4, 2)),
            dma((8, 2)),
            dma((8, 2)),
            dma((4,)),
            dma((4,)),
            dma((6,)),
            dma((6,)),
            dma((2,)),
            dma((2,)),
        ],
        compiler_params=pltpu.CompilerParams(
            collective_id=0, has_side_effects=True, vmem_limit_bytes=60 * 1024 * 1024
        ),
    )(query1, key1, value1, log_decay, out_weight, query2, key2, value2)


def solution(mesh):
    spec = P("ctx", "head")
    return jax.shard_map(
        per_device,
        mesh=mesh,
        in_specs=(spec, spec, spec, spec, P("head", None), spec, spec, spec),
        out_specs=(P(("ctx", "head"), None), spec),
        check_vma=False,
    )
```

time: 306 us -> 92.3 us (0.30)
  the two profiles are of different devices: /device:TPU:1 before, /device:TPU:193 now
where the time goes in v1:
time: 92.3 us; the launch traced here: 92 us
  Pallas kernels  86 us (93%)
  local copies, waits for them, and re-layouts  5.38 us (6%)
    pallas_call x1, Pallas kernels, per_device(): pl.pallas_call(kernel, out_shape=(jax.ShapeDtypeStruct((64, PROJ), BF16),...  86 us
    unnamed x3, local copies, waits for them, and re-layouts  5.38 us

profile of v1, /device:TPU:193, one launch (start us, length us, event | category | flops | bytes accessed | tf_op | source)
XLA Modules:
  0.0 92.0 jit_solution(17015664560164827665)
XLA Ops:
  0.6 1.6 %copy.10.dec = f32[512,8]{1,0:T(8,128)} copy(f32[512,8]{0,1:T(8,128)} %param.11) | data formatting | bytes 32768 | tf_op args[3]
  2.2 86.0 %shard_map.95 = (bf16[64,3072]{1,0:T(8,128)(2,1)}, bf16[512,768]{1,0:T(8,128)(2,1)}) custom-call(bf16[512,768]{1,0:T(8,128)(2,1)} %q1h.1, bf16[512,768]{1,0:T(8,128)(2,1)} %k1h.1, bf16[512,768]{1,0:T(8,128)(2,1)} %v1h.1, f32[512,8]{1,0:T(8,128)} %copy.10.dec, bf16[768,3072]{1,0:T(8,128)(2,1)} %wh.1, bf16[512,768]{1,0:T(8,128)(2,1)} %q2h.1, ...), custom_call_target="tpu_custom_call" | custom-call | tf_op jit(solution)/shard_map/pallas_call | solution.py:515
  88.2 1.8 %copy.13 = bf16[64,3072]{1,0:T(8,128)(2,1)} copy(bf16[64,3072]{1,0:T(8,128)(2,1)} %get-tuple-element.4) | data formatting | bytes 786432
  89.9 2.1 %copy.14 = bf16[512,768]{1,0:T(8,128)(2,1)} copy(bf16[512,768]{1,0:T(8,128)(2,1)} %get-tuple-element.5) | data formatting | bytes 1572864

commit v2 on v1

v2 whole, which is shorter than its diff:
```python
import math

import jax
import jax.numpy as jnp
from jax import lax
from jax.experimental import pallas as pl
from jax.experimental.pallas import tpu as pltpu
from jax.sharding import PartitionSpec as P

DH = 96
ROWS = 512
COLS = 768
NH = 8
GW = 384
PROJ = 3072
WIN = 256
SPAN = 1792
NEG = -1e30
EPS = 1e-6
MESH = pl.DeviceIdType.MESH
F32 = jnp.float32
BF16 = jnp.bfloat16
HBM = pltpu.MemorySpace.HBM

HALO_AFTER_A = [(0, 1, 0), (1, 0, 0)]
HALO_AFTER_B = [(1, 1, 0)]
HALO_AFTER_C = [(0, 0, 0), (0, 1, 1), (1, 0, 1), (0, 0, 1), (1, 1, 1)]
MSG = 112
STEP = 512


def dot(a, b, ca, cb):
    return lax.dot_general(a, b, (((ca,), (cb,)), ((), ())), preferred_element_type=F32)


def lanes(shape):
    return lax.broadcasted_iota(jnp.int32, shape, len(shape) - 1)


def rows_of(shape):
    return lax.broadcasted_iota(jnp.int32, shape, len(shape) - 2)


def head_window(h):
    start = GW * lax.div(h, 4) + 128 * lax.div(lax.rem(h, 4), 2)
    return pl.multiple_of(start, 128), DH * h - start


def head_mask(low):
    lane = lanes((1, WIN))
    return (lane >= low) & (lane < low + DH)


def same_head(tile):
    row = lax.div(rows_of((GW, 128)), DH)
    col = lax.div(lanes((GW, 128)) + 128 * tile, DH)
    return row == col


def kernel(
    q1h, k1h, v1h, dec, wh, q2h, k2h, v2h,
    lin_out, att_out,
    q1, k1, v1, q2, kk, vv, w,
    crow, ct, cexp, acc, fold, recv_a, tot_b, recv_b, pacc, send_c, recv_c,
    normed, own_part, pass_part, x1s, x1r, x2s, x2r, ys, yr,
    s_scr, p_scr,
    load_sem, halo_send, halo_recv, fwd_send, relay_send, a_send, a_recv, b_send, b_recv, c_send, c_recv,
    x1_send, x1_recv, x2_send, x2_recv, y_send, y_recv,
):
    t, hd = lax.axis_index("ctx"), lax.axis_index("head")
    core, y_hi = lax.rem(t, 2), lax.rem(lax.div(t, 2), 2)
    group, me = lax.div(t, 8), lax.rem(t, 8)
    yl, x = lax.div(hd, 4), lax.rem(hd, 4)
    sibling = t + 1 - 2 * core
    x_to = (yl * 4 + lax.rem(x + 1, 4), yl * 4 + lax.rem(x + 3, 4))
    y_other = (1 - yl) * 4 + x

    related = [
        (lax.rem(t + 2, 32), hd),
        (lax.rem(t + 30, 32), hd),
        (lax.rem(t + 4, 32), hd),
        (lax.rem(t + 28, 32), hd),
        (lax.rem(t + 29 + 6 * core, 32), hd),
        (t, x_to[0]),
        (t, x_to[1]),
        (t, y_other),
    ]
    related += [(8 * group + lax.rem(me + d, 8), hd) for d in range(1, 8)]
    related += [(lax.rem(t + 8 * d, 32), hd) for d in range(1, 4)]
    barrier = pltpu.get_barrier_semaphore()
    for device in related:
        pl.semaphore_signal(barrier, inc=1, device_id=device, device_id_type=MESH)

    own = pl.ds(3 * ROWS, ROWS)
    loads = [
        pltpu.make_async_copy(src, dst, load_sem.at[i])
        for i, (src, dst) in enumerate(
            [(k1h, k1), (v1h, v1), (q1h, q1), (q2h, q2), (k2h, kk.at[own]), (v2h, vv.at[own]), (wh, w)]
        )
    ]
    for copy in loads:
        copy.start()

    def half(g):
        return pl.ds(GW * g, GW)

    def block(slot):
        return pl.ds(pl.multiple_of(slot * ROWS, ROWS), ROWS)

    def halo(kind, kv, g):
        src, dst = ((k2h, kk), (v2h, vv))[kv]
        if kind == 1:
            slot, sem, target = 2 - 2 * core, 2 - 2 * core, lax.rem(t + 1 + 2 * core, 32)
        elif kv == 1:
            slot, sem, target = 1 + 3 * y_hi, 1 + 2 * y_hi, t + 2 - 4 * y_hi
        else:
            slot, sem, target = 1, 1, lax.rem(t + 2, 32)
        return pltpu.make_async_remote_copy(
            src_ref=src.at[:, half(g)],
            dst_ref=dst.at[block(slot), half(g)],
            send_sem=halo_send.at[kind, kv, g],
            recv_sem=halo_recv.at[sem, kv, g],
            device_id=(target, hd),
            device_id_type=MESH,
        )

    def arrived(sem, kv, g):
        dst = (kk, vv)[kv].at[pl.ds((4 if sem == 3 else sem) * ROWS, ROWS), half(g)]
        return pltpu.make_async_remote_copy(
            src_ref=dst,
            dst_ref=dst,
            send_sem=halo_send.at[0, kv, g],
            recv_sem=halo_recv.at[sem, kv, g],
            device_id=(sibling, hd),
            device_id_type=MESH,
        )

    def forward(kv, g):
        buf = (kk, vv)[kv]
        return pltpu.make_async_remote_copy(
            src_ref=buf.at[pl.ds(ROWS, ROWS), half(g)],
            dst_ref=buf.at[block(2 * core), half(g)],
            send_sem=fwd_send.at[kv, g],
            recv_sem=halo_recv.at[2 * core, kv, g],
            device_id=(sibling, hd),
            device_id_type=MESH,
        )

    def relay(g):
        return pltpu.make_async_remote_copy(
            src_ref=vv.at[pl.ds(4 * ROWS, ROWS), half(g)],
            dst_ref=vv.at[pl.ds(ROWS, ROWS), half(g)],
            send_sem=relay_send.at[g],
            recv_sem=halo_recv.at[1, 1, g],
            device_id=(lax.rem(t + 4, 32), hd),
            device_id_type=MESH,
        )

    def relay_on(g):
        @pl.when(y_hi == 0)
        def _():
            arrived(3, 1, g).wait_recv()
            relay(g).start()

    ct[...] = lax.dot_general(
        dec[...],
        (rows_of((ROWS, ROWS)) <= lanes((ROWS, ROWS))).astype(F32),
        (((1,), (0,)), ((), ())),
        precision=lax.Precision.HIGHEST,
        preferred_element_type=F32,
    )
    running = jnp.transpose(jnp.concatenate([ct[...], jnp.zeros((128 - NH, ROWS), F32)], axis=0))
    for h in range(NH):
        crow[h] = jnp.broadcast_to(running[:, h : h + 1], (ROWS, 128))
    lane = lanes((ROWS, 128))
    for g in range(2):
        for tile, cut in enumerate((96, 64, 32)):
            h = 4 * g + tile
            at = pl.ds(GW * g + 128 * tile, 128)
            cexp[:, at] = jnp.where(lane < cut, crow[h], crow[h + 1])

    def message(ref, index, state, decay):
        ref[index, :DH, :] = state.astype(BF16)
        high = decay.astype(BF16)
        rest = decay - high.astype(F32)
        middle = rest.astype(BF16)
        low = (rest - middle.astype(F32)).astype(BF16)
        row = rows_of((MSG - DH, 128))
        parts = [jnp.broadcast_to(p.astype(F32), (MSG - DH, 128)) for p in (high, middle, low)]
        tail = jnp.where(row == 0, parts[0], jnp.where(row == 1, parts[1], jnp.where(row == 2, parts[2], 0.0)))
        ref[index, DH:, :] = tail.astype(BF16)

    def decay_in(ref, index):
        return jnp.sum(ref[index, DH:, :].astype(F32), axis=0, keepdims=True)

    loads[0].wait()
    loads[1].wait()
    for g in range(2):
        c = cexp[:, half(g)]
        kw = (k1[:, half(g)].astype(F32) * jnp.exp(cexp[ROWS - 1 : ROWS, half(g)] - c)).astype(BF16)
        full = dot(kw, v1[:, half(g)], 0, 0)
        total = jnp.zeros((GW, 128), F32)
        for tile in range(3):
            total += jnp.where(same_head(tile), full[:, 128 * tile : 128 * tile + 128], 0.0)
        for i in range(4):
            h = 4 * g + i
            message(fold, h, total[DH * i : DH * i + DH], crow[h, ROWS - 1 : ROWS, :])

    pl.semaphore_wait(barrier, len(related))

    a_copies = []
    for d in range(1, 8):
        to = lax.rem(me + d, 8)
        copy = pltpu.make_async_remote_copy(
            src_ref=fold.at[to], dst_ref=recv_a.at[d], send_sem=a_send.at[d], recv_sem=a_recv.at[d],
            device_id=(8 * group + to, hd), device_id_type=MESH,
        )
        copy.start()
        a_copies.append(copy)
    recv_a[0] = fold[me]
    for item in HALO_AFTER_A:
        halo(*item).start()

    acc[...] = jnp.zeros_like(acc)
    loads[2].wait()
    tri = rows_of((256, 256)) >= lanes((256, 256))

    def intra(h, _):
        start, low = head_window(h)
        window = pl.ds(start, WIN)
        mask = head_mask(low)
        keep = mask.astype(F32).astype(BF16)
        qw = q1[:, window] * keep
        kw = k1[:, window]
        vw = v1[:, window]
        s0 = dot(qw[:256], kw[:256], 1, 1)
        s1 = dot(qw[256:], kw, 1, 1)
        ci = crow[h]
        ci = jnp.concatenate([ci, ci], axis=1)
        cj = ct[pl.ds(h, 1), :]
        e0 = jnp.exp(jnp.where(tri, ci[:256] - cj[:, :256], NEG))
        e10 = jnp.exp(ci[256:] - cj[:, :256])
        e11 = jnp.exp(jnp.where(tri, ci[256:] - cj[:, 256:], NEG))
        m0 = (s0 * e0).astype(BF16)
        m1 = (s1 * jnp.concatenate([e10, e11], axis=1)).astype(BF16)
        acc[pl.ds(0, 256), window] = jnp.where(mask, dot(m0, vw[:256], 1, 0), acc[pl.ds(0, 256), window])
        acc[pl.ds(256, 256), window] = jnp.where(mask, dot(m1, vw, 1, 0), acc[pl.ds(256, 256), window])
        return 0

    lax.fori_loop(0, NH // 2, intra, 0)

    for copy in a_copies:
        copy.wait_recv()

    def member(i):
        return lax.rem(me + 8 - i, 8)

    def then(state, ref, index):
        return jnp.exp(decay_in(ref, index)) * state + ref[index, :DH, :].astype(F32)

    total = jnp.zeros((DH, 128), F32)
    decay = jnp.zeros((1, 128), F32)
    for i in range(8):
        total = then(total, recv_a, member(i))
        decay = decay + decay_in(recv_a, i)
    message(tot_b, 0, total, decay)
    b_copies = []
    for d in range(1, 4):
        copy = pltpu.make_async_remote_copy(
            src_ref=tot_b.at[0], dst_ref=recv_b.at[d], send_sem=b_send.at[d], recv_sem=b_recv.at[d],
            device_id=(lax.rem(t + 8 * d, 32), hd), device_id_type=MESH,
        )
        b_copies.append(copy)

        @pl.when(group + d < 4)
        def _(copy=copy):
            copy.start()

    for item in HALO_AFTER_B:
        halo(*item).start()

    lax.fori_loop(NH // 2, NH, intra, 0)

    pacc[...] = jnp.zeros_like(pacc)
    for d in range(3, 0, -1):

        @pl.when(group >= d)
        def _(d=d):
            b_copies[d - 1].wait_recv()
            pacc[...] = then(pacc[...], recv_b, d)

    state = pacc[...]
    for i in range(8):
        send_c[i] = state.astype(BF16)
        if i < 7:
            state = then(state, recv_a, member(i))
    c_copies = []
    for d in range(1, 8):
        to = lax.rem(me + d, 8)
        copy = pltpu.make_async_remote_copy(
            src_ref=send_c.at[to], dst_ref=recv_c.at[me], send_sem=c_send.at[d], recv_sem=c_recv.at[d],
            device_id=(8 * group + to, hd), device_id_type=MESH,
        )
        copy.start()
        c_copies.append(copy)
    recv_c[me] = send_c[me]
    for item in HALO_AFTER_C:
        halo(*item).start()
    loads[6].wait()
    relay_on(0)
    for copy in c_copies:
        copy.wait_recv()

    for g in range(2):
        states = jnp.concatenate([recv_c[4 * g + i] for i in range(4)], axis=0).astype(F32)
        wide = jnp.concatenate([jnp.where(same_head(i), states, 0.0).astype(BF16) for i in range(3)], axis=1)
        ones = jnp.concatenate([same_head(i).astype(F32).astype(BF16) for i in range(3)], axis=1)
        both = dot(q1[:, half(g)], wide, 1, 0) * jnp.exp(cexp[:, half(g)]) + acc[:, half(g)]
        square = both * both
        high = square.astype(BF16)
        rest = (square - high.astype(F32)).astype(BF16)
        mean = (dot(high, ones, 1, 0) + dot(rest, ones, 1, 0)) * (1.0 / DH)
        normed[:, half(g)] = (both * lax.rsqrt(mean + EPS)).astype(BF16)

    def cols_at(i):
        return pl.ds(pl.multiple_of(STEP * i, STEP), STEP)

    def project(d, i):
        xt = lax.rem(x + d, 4)
        a = jnp.concatenate(
            [
                normed[pl.ds(pl.multiple_of(64 * xt, 64), 64), :],
                normed[pl.ds(pl.multiple_of(256 + 64 * xt, 64), 64), :],
            ],
            axis=0,
        )
        return dot(a, w[:, cols_at(i)], 1, 0)

    def x1(side, c):
        return pltpu.make_async_remote_copy(
            src_ref=x1s.at[side, c], dst_ref=x1r.at[side, c], send_sem=x1_send.at[side, c], recv_sem=x1_recv.at[side, c],
            device_id=(t, x_to[side]), device_id_type=MESH,
        )

    def x2(to, i):
        return pltpu.make_async_remote_copy(
            src_ref=x2s.at[to, i], dst_ref=x2r.at[to, i], send_sem=x2_send.at[to, i], recv_sem=x2_recv.at[to, i],
            device_id=(t, x_to[to]), device_id_type=MESH,
        )

    def yc(side, c):
        return pltpu.make_async_remote_copy(
            src_ref=ys.at[side, c], dst_ref=yr.at[side, c], send_sem=y_send.at[side, c], recv_sem=y_recv.at[side, c],
            device_id=(t, y_other), device_id_type=MESH,
        )

    def first(c, _):
        for side in range(2):
            x1s[side, c] = project(2, c + 3 * side).astype(BF16)
            x1(side, c).start()
        return 0

    def alone(c, _):
        for side in range(2):
            x2s[side, c + 3 - 3 * side] = project(1 + 2 * side, c + 3 - 3 * side).astype(BF16)
        return 0

    def kept(c, _):
        for side in range(2):
            pass_part[side, c] = project(1 + 2 * side, c + 3 * side)
        return 0

    def mine(i, _):
        own_part[i] = project(0, i)
        return 0

    lax.fori_loop(0, 3, first, 0)
    lax.fori_loop(0, 3, alone, 0)
    for side in range(2):
        x2(side, 3 - 3 * side).start()
    lax.fori_loop(0, 3, kept, 0)
    lax.fori_loop(0, 6, mine, 0)

    def second(c):
        for side in range(2):
            x1(side, c).wait_recv()
            x2s[side, c + 3 * side] = (pass_part[side, c] + x1r[side, c].astype(F32)).astype(BF16)
            x2(side, c + 3 * side).start()
        if c < 2:
            for side in range(2):
                x2(side, c + 1 + 3 - 3 * side).start()

    mine_rows = pl.ds(pl.multiple_of(64 * yl, 64), 64)
    their_rows = pl.ds(pl.multiple_of(64 * (1 - yl), 64), 64)

    def third(c):
        for side in range(2):
            i = c + 3 * side
            x2(0, i).wait_recv()
            x2(1, i).wait_recv()

            def total(rows):
                return own_part[i, rows] + x2r[0, i, rows].astype(F32) + x2r[1, i, rows].astype(F32)

            ys[side, c] = total(their_rows).astype(BF16)
            yc(side, c).start()
            own_part[i, mine_rows] = total(mine_rows)

    def last(c):
        for side in range(2):
            i = c + 3 * side
            yc(side, c).wait_recv()
            lin_out[:, pl.ds(STEP * i, STEP)] = (own_part[i, mine_rows] + yr[side, c].astype(F32)).astype(BF16)

    def pass_on(g):
        for kv in range(2):
            arrived(1, kv, g).wait_recv()
            forward(kv, g).start()

    def need(g):
        for kv in range(2):
            for slot in (0, 2):
                arrived(slot, kv, g).wait_recv()

    scale = (1.0 / math.sqrt(DH)) * math.log2(math.e)
    upper = lanes((256, 256)) > rows_of((256, 256))

    def attend(h, _):
        start, low = head_window(h)
        window = pl.ds(start, WIN)
        mask = head_mask(low)
        keep = mask.astype(F32).astype(BF16)
        for i in range(2):
            keys = pl.ds(256 * i, SPAN)
            qw = q2[pl.ds(256 * i, 256), window] * keep
            s_scr[i] = dot(qw, kk[keys, window], 1, 1)
            tops = []
            for n in range(7):
                cols = pl.ds(256 * n, 256)
                if n == 0:
                    s_scr[i, :, cols] = jnp.where(upper, s_scr[i, :, cols], NEG)
                if n == 6:
                    s_scr[i, :, cols] = jnp.where(tri, s_scr[i, :, cols], NEG)
                block = s_scr[i, :, cols]
                top = jnp.maximum(block[:, :128], block[:, 128:])
                first = 3 - (i + n) // 2
                if first > 0:
                    top = jnp.minimum(top, jnp.where(t >= first, 1e38, -1e38))
                tops.append(top)
            while len(tops) > 1:
                tops = [jnp.maximum(*tops[n : n + 2]) if n + 1 < len(tops) else tops[n] for n in range(0, len(tops), 2)]
            peak = jnp.max(tops[0], axis=1, keepdims=True) * scale
            total = jnp.zeros((256, 128), F32)
            for n in range(7):
                cols = pl.ds(256 * n, 256)
                first = 3 - (i + n) // 2
                shift = peak + jnp.where(t >= first, 0.0, 1e30) if first > 0 else peak
                e = jnp.exp2(s_scr[i, :, cols] * scale - shift)
                total += e[:, :128] + e[:, 128:]
                p_scr[i, :, cols] = e.astype(BF16)
            out = dot(p_scr[i], vv[keys, window], 1, 0) * (1.0 / jnp.sum(total, axis=1, keepdims=True))
            rows = pl.ds(256 * i, 256)
            old = att_out[rows, window].astype(F32)
            att_out[rows, window] = jnp.where(mask, out, old).astype(BF16)
        return 0

    att_out[...] = jnp.zeros_like(att_out)
    for i in (3, 4, 5):
        loads[i].wait()
    pass_on(0)
    need(0)
    lax.fori_loop(0, 1, attend, 0)
    second(0)
    lax.fori_loop(1, 3, attend, 0)
    second(1)
    relay_on(1)
    lax.fori_loop(3, 4, attend, 0)
    second(2)
    third(0)
    pass_on(1)
    need(1)
    lax.fori_loop(4, 5, attend, 0)
    third(1)
    lax.fori_loop(5, 7, attend, 0)
    third(2)
    last(0)
    lax.fori_loop(7, 8, attend, 0)
    last(1)
    last(2)

    for item in HALO_AFTER_A + HALO_AFTER_B + HALO_AFTER_C:
        halo(*item).wait_send()
    for g in range(2):
        for kv in range(2):
            forward(kv, g).wait_send()

        @pl.when(y_hi == 0)
        def _(g=g):
            relay(g).wait_send()

    for copy in a_copies + c_copies:
        copy.wait_send()
    for side in range(2):
        for c in range(3):
            x1(side, c).wait_send()
            yc(side, c).wait_send()
        for i in range(6):
            x2(side, i).wait_send()
    for d in range(1, 4):

        @pl.when(group + d < 4)
        def _(copy=b_copies[d - 1]):
            copy.wait_send()


def per_device(query1, key1, value1, log_decay, out_weight, query2, key2, value2):
    vm = pltpu.VMEM
    dma = pltpu.SemaphoreType.DMA
    hbm = pl.BlockSpec(memory_space=HBM)
    vmem = pl.BlockSpec(memory_space=vm)
    return pl.pallas_call(
        kernel,
        out_shape=(
            jax.ShapeDtypeStruct((64, PROJ), BF16),
            jax.ShapeDtypeStruct((ROWS, COLS), BF16),
        ),
        in_specs=[hbm, hbm, hbm, vmem, hbm, hbm, hbm, hbm],
        out_specs=(vmem, vmem),
        scratch_shapes=[
            vm((ROWS, COLS), BF16),
            vm((ROWS, COLS), BF16),
            vm((ROWS, COLS), BF16),
            vm((ROWS, COLS), BF16),
            vm((4 * ROWS, COLS), BF16),
            vm((5 * ROWS, COLS), BF16),
            vm((COLS, PROJ), BF16),
            vm((NH, ROWS, 128), F32),
            vm((NH, ROWS), F32),
            vm((ROWS, COLS), F32),
            vm((ROWS, COLS), F32),
            vm((NH, MSG, 128), BF16),
            vm((8, MSG, 128), BF16),
            vm((1, MSG, 128), BF16),
            vm((4, MSG, 128), BF16),
            vm((DH, 128), F32),
            vm((8, DH, 128), BF16),
            vm((8, DH, 128), BF16),
            vm((ROWS, COLS), BF16),
            vm((6, 128, STEP), F32),
            vm((2, 3, 128, STEP), F32),
            vm((2, 3, 128, STEP), BF16),
            vm((2, 3, 128, STEP), BF16),
            vm((2, 6, 128, STEP), BF16),
            vm((2, 6, 128, STEP), BF16),
            vm((2, 3, 64, STEP), BF16),
            vm((2, 3, 64, STEP), BF16),
            vm((2, 256, SPAN), F32),
            vm((2, 256, SPAN), BF16),
            dma((7,)),
            dma((2, 2, 2)),
            dma((4, 2, 2)),
            dma((2, 2)),
            dma((2,)),
            dma((8,)),
            dma((8,)),
            dma((4,)),
            dma((4,)),
            dma((8,)),
            dma((8,)),
            dma((2, 3)),
            dma((2, 3)),
            dma((2, 6)),
            dma((2, 6)),
            dma((2, 3)),
            dma((2, 3)),
        ],
        compiler_params=pltpu.CompilerParams(
            collective_id=0, has_side_effects=True, vmem_limit_bytes=60 * 1024 * 1024
        ),
    )(query1, key1, value1, log_decay.T, out_weight, query2, key2, value2)


def solution(mesh):
    spec = P("ctx", "head")
    return jax.shard_map(
        per_device,
        mesh=mesh,
        in_specs=(spec, spec, spec, spec, P("head", None), spec, spec, spec),
        out_specs=(P(("ctx", "head"), None), spec),
        check_vma=False,
    )
```

time: 92.3 us -> 81.3 us (0.88)
  the two profiles are of different devices: /device:TPU:193 before, /device:TPU:1 now
where the time goes in v2:
time: 81.3 us; the launch traced here: 81.1 us
  Pallas kernels  76.6 us (94%)
  local copies, waits for them, and re-layouts  3.83 us (5%)
    pallas_call x1, Pallas kernels, per_device(): pl.pallas_call(kernel, out_shape=(jax.ShapeDtypeStruct((64, PROJ), BF16),...  76.6 us
    unnamed x2, local copies, waits for them, and re-layouts  3.83 us

profile of v2, /device:TPU:1, one launch (start us, length us, event | category | flops | bytes accessed | tf_op | source)
XLA Modules:
  0.0 81.1 jit_solution(12013260079365954238)
XLA Ops:
  0.6 76.6 %shard_map.95 = (bf16[64,3072]{1,0:T(8,128)(2,1)}, bf16[512,768]{1,0:T(8,128)(2,1)}) custom-call(bf16[512,768]{1,0:T(8,128)(2,1)} %q1h.1, bf16[512,768]{1,0:T(8,128)(2,1)} %k1h.1, bf16[512,768]{1,0:T(8,128)(2,1)} %v1h.1, f32[8,512]{1,0:T(8,128)} %bitcast.1, bf16[768,3072]{1,0:T(8,128)(2,1)} %wh.1, bf16[512,768]{1,0:T(8,128)(2,1)} %q2h.1, ...), custom_call_target="tpu_custom_call" | custom-call | tf_op jit(solution)/shard_map/pallas_call | solution.py:521
  77.2 1.8 %copy.12 = bf16[64,3072]{1,0:T(8,128)(2,1)} copy(bf16[64,3072]{1,0:T(8,128)(2,1)} %get-tuple-element.4) | data formatting | bytes 786432
  79.0 2.1 %copy.13 = bf16[512,768]{1,0:T(8,128)(2,1)} copy(bf16[512,768]{1,0:T(8,128)(2,1)} %get-tuple-element.5) | data formatting | bytes 1572864

commit v3 on v2

--- a/solution.py
+++ b/solution.py
@@ -22,9 +22,11 @@
 BF16 = jnp.bfloat16
 HBM = pltpu.MemorySpace.HBM
 
-HALO_AFTER_A = [(0, 1, 0), (1, 0, 0)]
-HALO_AFTER_B = [(1, 1, 0)]
-HALO_AFTER_C = [(0, 0, 0), (0, 1, 1), (1, 0, 1), (0, 0, 1), (1, 1, 1)]
+PIECES = ((0, 256, 0, 384), (256, 256, 0, 384), (0, 512, 384, 256), (0, 512, 640, 128))
+HALO_AFTER_A = [(0, 1, 0), (1, 0, 0), (0, 1, 1), (1, 0, 1)]
+HALO_AFTER_B = [(1, 1, 0), (0, 0, 0), (1, 1, 1)]
+HALO_AFTER_C = [(0, 1, 2), (0, 1, 3), (1, 0, 2), (0, 0, 1), (1, 1, 2), (0, 0, 2), (1, 0, 3), (0, 0, 3), (1, 1, 3)]
+VMEM_LIMIT = 60 * 1024 * 1024
 MSG = 112
 STEP = 512
 
@@ -104,10 +106,11 @@
     def half(g):
         return pl.ds(GW * g, GW)
 
-    def block(slot):
-        return pl.ds(pl.multiple_of(slot * ROWS, ROWS), ROWS)
-
-    def halo(kind, kv, g):
+    def piece(slot, n):
+        row, rows, col, cols = PIECES[n]
+        return pl.ds(pl.multiple_of(slot * ROWS + row, 256), rows), pl.ds(col, cols)
+
+    def halo(kind, kv, n):
         src, dst = ((k2h, kk), (v2h, vv))[kv]
         if kind == 1:
             slot, sem, target = 2 - 2 * core, 2 - 2 * core, lax.rem(t + 1 + 2 * core, 32)
@@ -116,51 +119,51 @@
         else:
             slot, sem, target = 1, 1, lax.rem(t + 2, 32)
         return pltpu.make_async_remote_copy(
-            src_ref=src.at[:, half(g)],
-            dst_ref=dst.at[block(slot), half(g)],
-            send_sem=halo_send.at[kind, kv, g],
-            recv_sem=halo_recv.at[sem, kv, g],
+            src_ref=src.at[piece(0, n)],
+            dst_ref=dst.at[piece(slot, n)],
+            send_sem=halo_send.at[kind, kv, n],
+            recv_sem=halo_recv.at[sem, kv, n],
             device_id=(target, hd),
             device_id_type=MESH,
         )
 
-    def arrived(sem, kv, g):
-        dst = (kk, vv)[kv].at[pl.ds((4 if sem == 3 else sem) * ROWS, ROWS), half(g)]
+    def arrived(sem, kv, n):
+        dst = (kk, vv)[kv].at[piece(4 if sem == 3 else sem, n)]
         return pltpu.make_async_remote_copy(
             src_ref=dst,
             dst_ref=dst,
-            send_sem=halo_send.at[0, kv, g],
-            recv_sem=halo_recv.at[sem, kv, g],
+            send_sem=halo_send.at[0, kv, n],
+            recv_sem=halo_recv.at[sem, kv, n],
             device_id=(sibling, hd),
             device_id_type=MESH,
         )
 
-    def forward(kv, g):
+    def forward(kv, n):
         buf = (kk, vv)[kv]
         return pltpu.make_async_remote_copy(
-            src_ref=buf.at[pl.ds(ROWS, ROWS), half(g)],
-            dst_ref=buf.at[block(2 * core), half(g)],
-            send_sem=fwd_send.at[kv, g],
-            recv_sem=halo_recv.at[2 * core, kv, g],
+            src_ref=buf.at[piece(1, n)],
+            dst_ref=buf.at[piece(2 * core, n)],
+            send_sem=fwd_send.at[kv, n],
+            recv_sem=halo_recv.at[2 * core, kv, n],
             device_id=(sibling, hd),
             device_id_type=MESH,
         )
 
-    def relay(g):
+    def relay(n):
         return pltpu.make_async_remote_copy(
-            src_ref=vv.at[pl.ds(4 * ROWS, ROWS), half(g)],
-            dst_ref=vv.at[pl.ds(ROWS, ROWS), half(g)],
-            send_sem=relay_send.at[g],
-            recv_sem=halo_recv.at[1, 1, g],
+            src_ref=vv.at[piece(4, n)],
+            dst_ref=vv.at[piece(1, n)],
+            send_sem=relay_send.at[n],
+            recv_sem=halo_recv.at[1, 1, n],
             device_id=(lax.rem(t + 4, 32), hd),
             device_id_type=MESH,
         )
 
-    def relay_on(g):
+    def relay_on(n):
         @pl.when(y_hi == 0)
         def _():
-            arrived(3, 1, g).wait_recv()
-            relay(g).start()
+            arrived(3, 1, n).wait_recv()
+            relay(n).start()
 
     ct[...] = lax.dot_general(
         dec[...],
@@ -308,6 +311,7 @@
         halo(*item).start()
     loads[6].wait()
     relay_on(0)
+    relay_on(1)
     for copy in c_copies:
         copy.wait_recv()
 
@@ -412,15 +416,14 @@
             yc(side, c).wait_recv()
             lin_out[:, pl.ds(STEP * i, STEP)] = (own_part[i, mine_rows] + yr[side, c].astype(F32)).astype(BF16)
 
-    def pass_on(g):
-        for kv in range(2):
-            arrived(1, kv, g).wait_recv()
-            forward(kv, g).start()
-
-    def need(g):
+    def pass_on(kv, n):
+        arrived(1, kv, n).wait_recv()
+        forward(kv, n).start()
+
+    def need(n):
         for kv in range(2):
             for slot in (0, 2):
-                arrived(slot, kv, g).wait_recv()
+                arrived(slot, kv, n).wait_recv()
 
     scale = (1.0 / math.sqrt(DH)) * math.log2(math.e)
     upper = lanes((256, 256)) > rows_of((256, 256))
@@ -467,36 +470,43 @@
     att_out[...] = jnp.zeros_like(att_out)
     for i in (3, 4, 5):
         loads[i].wait()
-    pass_on(0)
+    pass_on(1, 0)
+    pass_on(1, 1)
+    pass_on(0, 0)
+    relay_on(2)
+    second(0)
+    relay_on(3)
+    pass_on(0, 1)
     need(0)
-    lax.fori_loop(0, 1, attend, 0)
-    second(0)
-    lax.fori_loop(1, 3, attend, 0)
+    need(1)
+    lax.fori_loop(0, 2, attend, 0)
     second(1)
-    relay_on(1)
-    lax.fori_loop(3, 4, attend, 0)
+    pass_on(1, 2)
+    lax.fori_loop(2, 4, attend, 0)
     second(2)
+    pass_on(1, 3)
+    pass_on(0, 2)
+    need(2)
     third(0)
-    pass_on(1)
-    need(1)
-    lax.fori_loop(4, 5, attend, 0)
+    lax.fori_loop(4, 6, attend, 0)
+    pass_on(0, 3)
+    need(3)
     third(1)
-    lax.fori_loop(5, 7, attend, 0)
+    lax.fori_loop(6, 8, attend, 0)
     third(2)
     last(0)
-    lax.fori_loop(7, 8, attend, 0)
     last(1)
     last(2)
 
     for item in HALO_AFTER_A + HALO_AFTER_B + HALO_AFTER_C:
         halo(*item).wait_send()
-    for g in range(2):
+    for n in range(4):
         for kv in range(2):
-            forward(kv, g).wait_send()
+            forward(kv, n).wait_send()
 
         @pl.when(y_hi == 0)
-        def _(g=g):
-            relay(g).wait_send()
+        def _(n=n):
+            relay(n).wait_send()
 
     for copy in a_copies + c_copies:
         copy.wait_send()
@@ -557,10 +567,10 @@
             vm((2, 256, SPAN), F32),
             vm((2, 256, SPAN), BF16),
             dma((7,)),
-            dma((2, 2, 2)),
-            dma((4, 2, 2)),
-            dma((2, 2)),
-            dma((2,)),
+            dma((2, 2, 4)),
+            dma((4, 2, 4)),
+            dma((2, 4)),
+            dma((4,)),
             dma((8,)),
             dma((8,)),
             dma((4,)),
@@ -575,7 +585,7 @@
             dma((2, 3)),
         ],
         compiler_params=pltpu.CompilerParams(
-            collective_id=0, has_side_effects=True, vmem_limit_bytes=60 * 1024 * 1024
+            collective_id=0, has_side_effects=True, vmem_limit_bytes=VMEM_LIMIT
         ),
     )(query1, key1, value1, log_decay.T, out_weight, query2, key2, value2)
 

time: 81.3 us -> 84.8 us (1.043)
  Pallas kernels: 76.6 us -> 80.2 us
    pallas_call x1, Pallas kernels: 76.6 us -> 80.2 us  [per_device(): pl.pallas_call(kernel, out_shape=(jax.ShapeDtypeStruct((64, PROJ), BF16),...]
where the time goes in v3:
time: 84.8 us; the launch traced here: 84.6 us
  Pallas kernels  80.2 us (95%)
  local copies, waits for them, and re-layouts  3.83 us (5%)
    pallas_call x1, Pallas kernels, per_device(): pl.pallas_call(kernel, out_shape=(jax.ShapeDtypeStruct((64, PROJ), BF16),...  80.2 us
    unnamed x2, local copies, waits for them, and re-layouts  3.83 us

profile of v3, /device:TPU:1, one launch (start us, length us, event | category | flops | bytes accessed | tf_op | source)
XLA Modules:
  0.0 84.6 jit_solution(9419060897599424442)
XLA Ops:
  0.6 80.2 %shard_map.95 = (bf16[64,3072]{1,0:T(8,128)(2,1)}, bf16[512,768]{1,0:T(8,128)(2,1)}) custom-call(bf16[512,768]{1,0:T(8,128)(2,1)} %q1h.1, bf16[512,768]{1,0:T(8,128)(2,1)} %k1h.1, bf16[512,768]{1,0:T(8,128)(2,1)} %v1h.1, f32[8,512]{1,0:T(8,128)} %bitcast.1, bf16[768,3072]{1,0:T(8,128)(2,1)} %wh.1, bf16[512,768]{1,0:T(8,128)(2,1)} %q2h.1, ...), custom_call_target="tpu_custom_call" | custom-call | tf_op jit(solution)/shard_map/pallas_call | solution.py:531
  80.8 1.8 %copy.12 = bf16[64,3072]{1,0:T(8,128)(2,1)} copy(bf16[64,3072]{1,0:T(8,128)(2,1)} %get-tuple-element.4) | data formatting | bytes 786432
  82.6 2.1 %copy.13 = bf16[512,768]{1,0:T(8,128)(2,1)} copy(bf16[512,768]{1,0:T(8,128)(2,1)} %get-tuple-element.5) | data formatting | bytes 1572864

commit v4 on v2

--- a/solution.py
+++ b/solution.py
@@ -24,7 +24,7 @@
 
 HALO_AFTER_A = [(0, 1, 0), (1, 0, 0)]
 HALO_AFTER_B = [(1, 1, 0)]
-HALO_AFTER_C = [(0, 0, 0), (0, 1, 1), (1, 0, 1), (0, 0, 1), (1, 1, 1)]
+HALO_AFTER_C = [(0, 1, 1), (1, 0, 1)]
 MSG = 112
 STEP = 512
 
@@ -304,6 +304,10 @@
         copy.start()
         c_copies.append(copy)
     recv_c[me] = send_c[me]
+    @pl.when(y_hi == 0)
+    def _():
+        halo(0, 0, 0).start()
+
     for item in HALO_AFTER_C:
         halo(*item).start()
     loads[6].wait()
@@ -375,6 +379,13 @@
         return 0
 
     lax.fori_loop(0, 3, first, 0)
+
+    @pl.when(y_hi == 1)
+    def _():
+        halo(0, 0, 0).start()
+
+    halo(0, 0, 1).start()
+    halo(1, 1, 1).start()
     lax.fori_loop(0, 3, alone, 0)
     for side in range(2):
         x2(side, 3 - 3 * side).start()
@@ -467,28 +478,26 @@
     att_out[...] = jnp.zeros_like(att_out)
     for i in (3, 4, 5):
         loads[i].wait()
+    second(0)
     pass_on(0)
-    need(0)
-    lax.fori_loop(0, 1, attend, 0)
-    second(0)
-    lax.fori_loop(1, 3, attend, 0)
     second(1)
     relay_on(1)
+    second(2)
+    need(0)
+    lax.fori_loop(0, 3, attend, 0)
+    third(0)
     lax.fori_loop(3, 4, attend, 0)
-    second(2)
-    third(0)
     pass_on(1)
     need(1)
-    lax.fori_loop(4, 5, attend, 0)
     third(1)
-    lax.fori_loop(5, 7, attend, 0)
+    lax.fori_loop(4, 6, attend, 0)
     third(2)
+    lax.fori_loop(6, 8, attend, 0)
     last(0)
-    lax.fori_loop(7, 8, attend, 0)
     last(1)
     last(2)
 
-    for item in HALO_AFTER_A + HALO_AFTER_B + HALO_AFTER_C:
+    for item in HALO_AFTER_A + HALO_AFTER_B + HALO_AFTER_C + [(0, 0, 0), (0, 0, 1), (1, 1, 1)]:
         halo(*item).wait_send()
     for g in range(2):
         for kv in range(2):
@@ -575,7 +584,7 @@
             dma((2, 3)),
         ],
         compiler_params=pltpu.CompilerParams(
-            collective_id=0, has_side_effects=True, vmem_limit_bytes=60 * 1024 * 1024
+            collective_id=0, has_side_effects=True, vmem_limit_bytes=53 * 1024 * 1024
         ),
     )(query1, key1, value1, log_decay.T, out_weight, query2, key2, value2)
 

time: 81.3 us -> 78.9 us (0.970)
  Pallas kernels: 76.6 us -> 74.6 us
    pallas_call x1, Pallas kernels: 76.6 us -> 74.6 us  [per_device(): pl.pallas_call(kernel, out_shape=(jax.ShapeDtypeStruct((64, PROJ), BF16),...]
    unnamed x2 -> x4, local copies, waits for them, and re-layouts: 3.83 us -> 3.52 us
where the time goes in v4:
time: 78.9 us; the launch traced here: 78.7 us
  Pallas kernels  74.6 us (95%)
  local copies, waits for them, and re-layouts  3.52 us (4%)
    pallas_call x1, Pallas kernels, per_device(): pl.pallas_call(kernel, out_shape=(jax.ShapeDtypeStruct((64, PROJ), BF16),...  74.6 us
    unnamed x4, local copies, waits for them, and re-layouts  3.52 us

profile of v4, /device:TPU:1, one launch (start us, length us, event | category | flops | bytes accessed | tf_op | source)
XLA Modules:
  0.0 78.7 jit_solution(10949633776655493984)
XLA Ops:
  0.6 0.0 copy-start
  0.6 0.7 copy-done
  1.4 74.6 %shard_map.95 = (bf16[64,3072]{1,0:T(8,128)(2,1)S(1)}, bf16[512,768]{1,0:T(8,128)(2,1)}) custom-call(bf16[512,768]{1,0:T(8,128)(2,1)} %q1h.1, bf16[512,768]{1,0:T(8,128)(2,1)} %k1h.1, bf16[512,768]{1,0:T(8,128)(2,1)} %v1h.1, f32[8,512]{1,0:T(8,128)S(1)} %bitcast.1, bf16[768,3072]{1,0:T(8,128)(2,1)} %wh.1, bf16[512,768]{1,0:T(8,128)(2,1)} %q2h.1, ...), custom_call_target="tpu_custom_call" | custom-call | tf_op jit(solution)/shard_map/pallas_call | solution.py:530
  75.9 0.7 copy.12
  76.7 2.1 %copy.13 = bf16[512,768]{1,0:T(8,128)(2,1)} copy(bf16[512,768]{1,0:T(8,128)(2,1)} %get-tuple-element.5) | data formatting | bytes 1572864
Async XLA Ops:
  0.6 0.7 copy-start

commit v5 on v4

--- a/solution.py
+++ b/solution.py
@@ -107,60 +107,65 @@
     def block(slot):
         return pl.ds(pl.multiple_of(slot * ROWS, ROWS), ROWS)
 
-    def halo(kind, kv, g):
+    def piece(slot, kv, n):
+        rows = 256 if kv == 1 and n > 0 else ROWS
+        start = slot * ROWS + (256 if n == 2 else 0)
+        return pl.ds(pl.multiple_of(start, 256), rows), half(min(n, 1))
+
+    def halo(kind, kv, n):
         src, dst = ((k2h, kk), (v2h, vv))[kv]
         if kind == 1:
             slot, sem, target = 2 - 2 * core, 2 - 2 * core, lax.rem(t + 1 + 2 * core, 32)
-        elif kv == 1:
+        elif kv == 1 and n < 2:
             slot, sem, target = 1 + 3 * y_hi, 1 + 2 * y_hi, t + 2 - 4 * y_hi
         else:
             slot, sem, target = 1, 1, lax.rem(t + 2, 32)
         return pltpu.make_async_remote_copy(
-            src_ref=src.at[:, half(g)],
-            dst_ref=dst.at[block(slot), half(g)],
-            send_sem=halo_send.at[kind, kv, g],
-            recv_sem=halo_recv.at[sem, kv, g],
+            src_ref=src.at[piece(0, kv, n)],
+            dst_ref=dst.at[piece(slot, kv, n)],
+            send_sem=halo_send.at[kind, kv, n],
+            recv_sem=halo_recv.at[sem, kv, n],
             device_id=(target, hd),
             device_id_type=MESH,
         )
 
-    def arrived(sem, kv, g):
-        dst = (kk, vv)[kv].at[pl.ds((4 if sem == 3 else sem) * ROWS, ROWS), half(g)]
+    def arrived(sem, kv, n):
+        dst = (kk, vv)[kv].at[piece(4 if sem == 3 else sem, kv, n)]
         return pltpu.make_async_remote_copy(
             src_ref=dst,
             dst_ref=dst,
-            send_sem=halo_send.at[0, kv, g],
-            recv_sem=halo_recv.at[sem, kv, g],
+            send_sem=halo_send.at[0, kv, n],
+            recv_sem=halo_recv.at[sem, kv, n],
             device_id=(sibling, hd),
             device_id_type=MESH,
         )
 
-    def forward(kv, g):
+    def forward(kv, n):
         buf = (kk, vv)[kv]
         return pltpu.make_async_remote_copy(
-            src_ref=buf.at[pl.ds(ROWS, ROWS), half(g)],
-            dst_ref=buf.at[block(2 * core), half(g)],
-            send_sem=fwd_send.at[kv, g],
-            recv_sem=halo_recv.at[2 * core, kv, g],
+            src_ref=buf.at[piece(1, kv, n)],
+            dst_ref=buf.at[piece(2 * core, kv, n)],
+            send_sem=fwd_send.at[kv, n],
+            recv_sem=halo_recv.at[2 * core, kv, n],
             device_id=(sibling, hd),
             device_id_type=MESH,
         )
 
-    def relay(g):
+    def relay(n):
         return pltpu.make_async_remote_copy(
-            src_ref=vv.at[pl.ds(4 * ROWS, ROWS), half(g)],
-            dst_ref=vv.at[pl.ds(ROWS, ROWS), half(g)],
-            send_sem=relay_send.at[g],
-            recv_sem=halo_recv.at[1, 1, g],
+            src_ref=vv.at[piece(4, 1, n)],
+            dst_ref=vv.at[piece(1, 1, n)],
+            send_sem=relay_send.at[n],
+            recv_sem=halo_recv.at[1, 1, n],
             device_id=(lax.rem(t + 4, 32), hd),
             device_id_type=MESH,
         )
 
-    def relay_on(g):
+    def relay_on(n):
         @pl.when(y_hi == 0)
         def _():
-            arrived(3, 1, g).wait_recv()
-            relay(g).start()
+            arrived(3, 1, n).wait_recv()
+            relay(n).start()
 
     ct[...] = lax.dot_general(
         dec[...],
@@ -384,8 +389,10 @@
     def _():
         halo(0, 0, 0).start()
 
+    halo(0, 1, 2).start()
+    halo(1, 1, 1).start()
     halo(0, 0, 1).start()
-    halo(1, 1, 1).start()
+    halo(1, 1, 2).start()
     lax.fori_loop(0, 3, alone, 0)
     for side in range(2):
         x2(side, 3 - 3 * side).start()
@@ -424,14 +431,14 @@
             lin_out[:, pl.ds(STEP * i, STEP)] = (own_part[i, mine_rows] + yr[side, c].astype(F32)).astype(BF16)
 
     def pass_on(g):
-        for kv in range(2):
-            arrived(1, kv, g).wait_recv()
-            forward(kv, g).start()
+        for kv, n in ((1, 0), (0, 0)) if g == 0 else ((1, 1), (1, 2), (0, 1)):
+            arrived(1, kv, n).wait_recv()
+            forward(kv, n).start()
 
     def need(g):
-        for kv in range(2):
+        for kv, n in ((1, 0), (0, 0)) if g == 0 else ((1, 1), (1, 2), (0, 1)):
             for slot in (0, 2):
-                arrived(slot, kv, g).wait_recv()
+                arrived(slot, kv, n).wait_recv()
 
     scale = (1.0 / math.sqrt(DH)) * math.log2(math.e)
     upper = lanes((256, 256)) > rows_of((256, 256))
@@ -497,15 +504,15 @@
     last(1)
     last(2)
 
-    for item in HALO_AFTER_A + HALO_AFTER_B + HALO_AFTER_C + [(0, 0, 0), (0, 0, 1), (1, 1, 1)]:
+    for item in HALO_AFTER_A + HALO_AFTER_B + HALO_AFTER_C + [(0, 0, 0), (0, 1, 2), (1, 1, 1), (0, 0, 1), (1, 1, 2)]:
         halo(*item).wait_send()
-    for g in range(2):
-        for kv in range(2):
-            forward(kv, g).wait_send()
+    for kv, n in ((0, 0), (0, 1), (1, 0), (1, 1), (1, 2)):
+        forward(kv, n).wait_send()
+    for n in range(2):
 
         @pl.when(y_hi == 0)
-        def _(g=g):
-            relay(g).wait_send()
+        def _(n=n):
+            relay(n).wait_send()
 
     for copy in a_copies + c_copies:
         copy.wait_send()
@@ -566,9 +573,9 @@
             vm((2, 256, SPAN), F32),
             vm((2, 256, SPAN), BF16),
             dma((7,)),
-            dma((2, 2, 2)),
-            dma((4, 2, 2)),
-            dma((2, 2)),
+            dma((2, 2, 3)),
+            dma((4, 2, 3)),
+            dma((2, 3)),
             dma((2,)),
             dma((8,)),
             dma((8,)),

time: 78.9 us -> 73.7 us (0.934)
  Pallas kernels: 74.6 us -> 69.3 us
    pallas_call x1, Pallas kernels: 74.6 us -> 69.3 us  [per_device(): pl.pallas_call(kernel, out_shape=(jax.ShapeDtypeStruct((64, PROJ), BF16),...]
where the time goes in v5:
time: 73.7 us; the launch traced here: 73.4 us
  Pallas kernels  69.3 us (94%)
  local copies, waits for them, and re-layouts  3.52 us (5%)
    pallas_call x1, Pallas kernels, per_device(): pl.pallas_call(kernel, out_shape=(jax.ShapeDtypeStruct((64, PROJ), BF16),...  69.3 us
    unnamed x4, local copies, waits for them, and re-layouts  3.52 us

profile of v5, /device:TPU:1, one launch (start us, length us, event | category | flops | bytes accessed | tf_op | source)
XLA Modules:
  0.0 73.4 jit_solution(7511420948257892066)
XLA Ops:
  0.6 0.0 copy-start
  0.6 0.7 copy-done
  1.4 69.3 %shard_map.95 = (bf16[64,3072]{1,0:T(8,128)(2,1)S(1)}, bf16[512,768]{1,0:T(8,128)(2,1)}) custom-call(bf16[512,768]{1,0:T(8,128)(2,1)} %q1h.1, bf16[512,768]{1,0:T(8,128)(2,1)} %k1h.1, bf16[512,768]{1,0:T(8,128)(2,1)} %v1h.1, f32[8,512]{1,0:T(8,128)S(1)} %bitcast.1, bf16[768,3072]{1,0:T(8,128)(2,1)} %wh.1, bf16[512,768]{1,0:T(8,128)(2,1)} %q2h.1, ...), custom_call_target="tpu_custom_call" | custom-call | tf_op jit(solution)/shard_map/pallas_call | solution.py:537
  70.6 0.7 %copy.12 = bf16[64,3072]{1,0:T(8,128)(2,1)} copy(bf16[64,3072]{1,0:T(8,128)(2,1)S(1)} %get-tuple-element.4) | data formatting | bytes 786432
  71.4 2.1 %copy.13 = bf16[512,768]{1,0:T(8,128)(2,1)} copy(bf16[512,768]{1,0:T(8,128)(2,1)} %get-tuple-element.5) | data formatting | bytes 1572864
Async XLA Ops:
  0.6 0.7 copy-start
